TPU v7x, 256 devices: a whole 4x4x8 slice. The times are simulated.
256 devices in a mesh: seq: 64 (over y, x, z_hi, core), fsdp: 4 (over z_lo).
Axes of the slice: x: 4, y: 4, z: 8 (z_hi: 2, z_lo: 4; z = z_hi * 4 + z_lo), core: 2. Of those that a mesh axis runs over, the one named last changes fastest.
Arguments:
- tokens: bfloat16 [40960, 5120], P('seq', 'fsdp'), may hold values from -24 to 24
- w_local: bfloat16 [5120, 3, 1536], P('seq', None, 'fsdp'), may hold values from -0.078125 to 0.078125
- w_strided: bfloat16 [5120, 3, 1024], P('seq', None, 'fsdp'), may hold values from -0.078125 to 0.078125
- valid: int32 [64, 640], P('seq'), may hold values 0 or 1
- band_reach: int32 [12], P('fsdp'), may hold values from 1 to 4, as said below
Outputs:
- out_local: bfloat16 [40960, 1536], P('seq', 'fsdp')
- out_strided: bfloat16 [40960, 1024], P('seq', 'fsdp')
Inputs may be any that keep to these rules, and one draw needn't show every extreme that they name: Query block b of local head h sees band blocks b - band_reach[h] to b.
All inputs are finite; a program needn't handle non-finite values. No bound on the sum of `valid` on one device may be relied on, other than what follows from the above.
Results may differ from a plain program's by a relative error of at most 0.012.
The roundings to bfloat16 on the way count: a program that leaves them out, or rounds other values in their place, can miss the bound.
Values may be sent and summed in bfloat16 or wider, within the bound.
No kernel may reach another device: no remote copies, remote signals or barrier semaphores. Data moves between devices by JAX's collectives and lax.ppermute only.
A program may use at most 128 MiB of HBM per device.

v0:
```python
import math
import jax
import jax.numpy as jnp
from jax import lax
from jax.sharding import PartitionSpec as P

HD = 128
BLK = 128


def local_attend(qkv_day, valid_day, reach, head_size):
    query = qkv_day[:, 0]
    keys = qkv_day[:, 1]
    values = qkv_day[:, 2]
    seconds = qkv_day.shape[0]
    scores = jnp.einsum(
        "qhc,khc->hqk", query, keys, preferred_element_type=jnp.float32
    ) / math.sqrt(head_size)
    position = jnp.arange(seconds)
    causal = position[None, :] <= position[:, None]
    block = position // BLK
    band = block[None, None, :] >= block[None, :, None] - reach[:, None, None]
    seen = (valid_day[None, :] > 0) | (position[None, :] == position[:, None])
    allowed = causal[None] & band & seen[None]
    scores = jnp.where(allowed, scores, -jnp.inf)
    row_max = jnp.max(scores, axis=-1, keepdims=True)
    expo = jnp.exp(scores - row_max)
    probs = (expo / jnp.sum(expo, axis=-1, keepdims=True)).astype(jnp.bfloat16)
    result = jnp.einsum("hqk,khc->qhc", probs, values, preferred_element_type=jnp.float32)
    return result.astype(jnp.bfloat16).reshape(seconds, -1)


def body(tokens, w_local, w_strided, valid, band_reach):
    gathered = lax.all_gather(tokens, "fsdp", axis=1, tiled=True)
    seconds = gathered.shape[0]
    local_cols = w_local.shape[2]
    strided_cols = w_strided.shape[2]
    head_size = HD
    peers = lax.axis_size("seq")
    per_peer = seconds // peers

    def add_rows(piece):
        rows = piece.shape[0]
        return jnp.dot(gathered, piece.reshape(rows, -1), preferred_element_type=jnp.float32)

    acc_local = add_rows(lax.all_gather(w_local, "seq", axis=0, tiled=True))
    acc_strided = add_rows(lax.all_gather(w_strided, "seq", axis=0, tiled=True))
    packed = acc_strided.astype(jnp.bfloat16).reshape(1, peers, per_peer, 3 * strided_cols)
    marks = valid.astype(jnp.bfloat16).reshape(1, peers, per_peer)
    strided_packed = lax.all_to_all(packed, "seq", split_axis=1, concat_axis=0, tiled=True)
    strided_marks = lax.all_to_all(marks, "seq", split_axis=1, concat_axis=0, tiled=True)
    days = strided_packed.shape[0]
    count = strided_packed.shape[2]
    heads = strided_cols // head_size
    split_up = strided_packed.reshape(days, count, 3, heads, head_size)
    query = split_up[:, :, 0]
    keys = split_up[:, :, 1]
    values = split_up[:, :, 2]
    scores = jnp.einsum(
        "dshc,eshc->shde", query, keys, preferred_element_type=jnp.float32
    ) / math.sqrt(head_size)
    day = jnp.arange(days)
    causal = day[None, :] <= day[:, None]
    same = day[None, :] == day[:, None]
    seen = jnp.transpose(strided_marks[:, 0, :]) > 0
    allowed = causal[None, None] & (seen[:, None, None, :] | same[None, None])
    scores = jnp.where(allowed, scores, -jnp.inf)
    row_max = jnp.max(scores, axis=-1, keepdims=True)
    expo = jnp.exp(scores - row_max)
    probs = (expo / jnp.sum(expo, axis=-1, keepdims=True)).astype(jnp.bfloat16)
    result = jnp.einsum("shde,eshc->dshc", probs, values, preferred_element_type=jnp.float32)
    result = result.astype(jnp.bfloat16).reshape(days, 1, count, strided_cols)
    result = lax.all_to_all(result, "seq", split_axis=0, concat_axis=1, tiled=True)
    out_strided = result.reshape(seconds, strided_cols)
    qkv_local = acc_local.astype(jnp.bfloat16).reshape(
        seconds, 3, local_cols // head_size, head_size
    )
    out_local = local_attend(qkv_local, valid[0], band_reach, head_size)
    return (out_local, out_strided)


def solution(mesh):
    in_specs = (
        P("seq", "fsdp"),
        P("seq", None, "fsdp"),
        P("seq", None, "fsdp"),
        P("seq", None),
        P("fsdp"),
    )
    out_specs = (P("seq", "fsdp"), P("seq", "fsdp"))
    return jax.shard_map(body, mesh=mesh, in_specs=in_specs, out_specs=out_specs, check_vma=False)
```

profile of v0, /device:TPU:1, one launch (start us, length us, event | category | flops | bytes accessed | tf_op | source)
XLA Modules:
  0.0 441.7 jit_solution(410772100073191428)
XLA Ops:
  7.2 0.7 all-gather.8.cloned.1.call-update
  7.9 0.7 all-gather.4.cloned.1.call-update
  9.4 0.7 convert_reduce_fusion
  10.1 0.8 reshape.195
  10.9 15.6 %all-to-all-start.1 = ((bf16[1,64,10]{2,0,1:T(2,128)(2,1)}), bf16[1,64,10]{2,0,1:T(2,128)(2,1)S(1)}, u32[]{:S(2)}, u32[]{:S(2)}) async-start(bf16[1,64,10]{2,0,1:T(2,128)(2,1)} %reshape.195), calls=%async_computation.1 | async-start | bytes 65536 | tf_op jit(solution)/shard_map/all_to_all | solution.py:51
  26.5 100.5 %all-gather.8.cloned.1.call-done = bf16[5120,3,256]{2,0,1:T(8,128)(2,1)} async-done(((bf16[80,3,256]{2,0,1:T(8,128)(2,1)}), bf16[5120,3,256]{2,0,1:T(8,128)(2,1)}) %all-gather.8.cloned.1.call-update) | async-done | bytes 7864336 | tf_op jit(solution)/shard_map/all_gather | solution.py:47
  127.0 11.0 %copy.51 = bf16[5120,3,256]{0,2,1:T(8,128)(2,1)} copy(bf16[5120,3,256]{2,0,1:T(8,128)(2,1)} %all-gather.8.cloned.1.call-done) | data formatting | bytes 15728640 | tf_op jit(solution)/shard_map/all_gather | solution.py:47
  138.0 107.3 %all-gather.4.cloned.1.call-done = bf16[640,5120]{1,0:T(8,128)(2,1)} async-done(((bf16[640,1280]{1,0:T(8,128)(2,1)}), bf16[640,5120]{1,0:T(8,128)(2,1)}) %all-gather.4.cloned.1.call-update) | async-done | bytes 6553616 | tf_op jit(solution)/shard_map/all_gather | solution.py:34
  245.3 9.7 %convolution_convert_fusion.1 = bf16[640,768]{1,0:T(8,128)(2,1)S(1)} fusion(bf16[640,5120]{1,0:T(8,128)(2,1)} %all-gather.4.cloned.1.call-done, bf16[5120,768]{0,1:T(8,128)(2,1)} %bitcast.60), kind=kOutput, calls=%fused_computation.17 | convolution fusion | flops 5033656320 | bytes 15400960 | tf_op jit(solution)/shard_map/dot_general | solution.py:44
  255.0 1.4 reshape.189
  256.4 11.4 %all-to-all-start = ((bf16[1,64,10,768]{3,2,0,1:T(8,128)(2,1)}), bf16[1,64,10,768]{3,2,0,1:T(8,128)(2,1)S(1)}, u32[]{:S(2)}, u32[]{:S(2)}) async-start(bf16[1,64,10,768]{3,2,0,1:T(8,128)(2,1)} %bitcast.8), calls=%async_computation | async-start | bytes 3145728 | tf_op jit(solution)/shard_map/all_to_all | solution.py:50
  268.2 37.1 %all-to-all-done = bf16[1,64,10,768]{3,2,0,1:T(8,128)(2,1)S(1)} async-done(((bf16[1,64,10,768]{3,2,0,1:T(8,128)(2,1)}), bf16[1,64,10,768]{3,2,0,1:T(8,128)(2,1)S(1)}, u32[]{:S(2)}, u32[]{:S(2)}) %all-to-all-start) | async-done | bytes 983072 | tf_op jit(solution)/shard_map/all_to_all | solution.py:50
  307.8 1.0 reshape.196
  308.8 4.4 all-to-all-start.2
  313.4 0.9 fusion.10
  314.3 14.2 %all-to-all-done.2 = bf16[64,1,10,256]{3,2,1,0:T(8,128)(2,1)S(1)} async-done(((bf16[64,1,10,256]{3,2,1,0:T(8,128)(2,1)}), bf16[64,1,10,256]{3,2,1,0:T(8,128)(2,1)S(1)}, u32[]{:S(2)}, u32[]{:S(2)}) %all-to-all-start.2) | async-done | bytes 327712 | tf_op jit(solution)/shard_map/all_to_all | solution.py:73
  328.5 0.8 reshape.193
  329.4 68.7 %all-gather.6.cloned.1.call-done = bf16[5120,3,384]{2,0,1:T(8,128)(2,1)} async-done(((bf16[80,3,384]{2,0,1:T(8,128)(2,1)}), bf16[5120,3,384]{2,0,1:T(8,128)(2,1)}) %all-gather.6.cloned.1.call-update) | async-done | bytes 11796496 | tf_op jit(solution)/shard_map/all_gather | solution.py:46
  398.1 15.0 %copy.46 = bf16[5120,3,384]{0,2,1:T(8,128)(2,1)} copy(bf16[5120,3,384]{2,0,1:T(8,128)(2,1)} %all-gather.6.cloned.1.call-done) | data formatting | bytes 23592960 | tf_op jit(solution)/shard_map/all_gather | solution.py:46
  413.1 12.7 %convolution_convert_fusion = bf16[640,1152]{1,0:T(8,128)(2,1)S(1)} fusion(bf16[640,5120]{1,0:T(8,128)(2,1)} %all-gather.4.cloned.1.call-done, bf16[5120,1152]{0,1:T(8,128)(2,1)} %bitcast.59), kind=kOutput, calls=%fused_computation.5 | convolution fusion | flops 7550484480 | bytes 19824640 | tf_op jit(solution)/shard_map/dot_general | solution.py:44
  425.8 0.9 copy.47
  426.7 3.5 fusion.31
  430.2 4.0 fusion.12
  434.2 1.0 copy.62
  (23 shorter events, 3.7 us)
Async XLA Ops:
  7.2 119.8 %all-gather.8.cloned.1.call-start = ((), (), s32[]{:S(2)}) async-start(), calls=%async_computation.5 | async-start | bytes 7987200 | tf_op jit(solution)/shard_map/all_gather | solution.py:47
  7.9 237.4 %all-gather.4.cloned.1.call-start = ((), (), s32[]{:S(2)}) async-start(), calls=%async_computation.3 | async-start | bytes 8192000 | tf_op jit(solution)/shard_map/all_gather | solution.py:34
  8.6 389.4 %all-gather.6.cloned.1.call-start = ((), (), s32[]{:S(2)}) async-start(), calls=%async_computation.4 | async-start | bytes 11980800 | tf_op jit(solution)/shard_map/all_gather | solution.py:46
  10.9 245.6 %all-to-all-start.1 = ((bf16[1,64,10]{2,0,1:T(2,128)(2,1)}), bf16[1,64,10]{2,0,1:T(2,128)(2,1)S(1)}, u32[]{:S(2)}, u32[]{:S(2)}) async-start(bf16[1,64,10]{2,0,1:T(2,128)(2,1)} %reshape.195), calls=%async_computation.1 | async-start | bytes 65536 | tf_op jit(solution)/shard_map/all_to_all | solution.py:51
  255.0 12.9 %copy-start = (s32[1,640]{1,0:T(1,128)S(1)}, s32[1,640]{1,0:T(1,128)}, u32[]{:S(2)}) copy-start(s32[1,640]{1,0:T(1,128)} %param.8) | copy-start | bytes 7684
  256.4 48.9 %all-to-all-start = ((bf16[1,64,10,768]{3,2,0,1:T(8,128)(2,1)}), bf16[1,64,10,768]{3,2,0,1:T(8,128)(2,1)S(1)}, u32[]{:S(2)}, u32[]{:S(2)}) async-start(bf16[1,64,10,768]{3,2,0,1:T(8,128)(2,1)} %bitcast.8), calls=%async_computation | async-start | bytes 3145728 | tf_op jit(solution)/shard_map/all_to_all | solution.py:50
  305.9 7.4 %copy-start.1 = (s32[3]{0:T(128)S(1)}, s32[3]{0:T(128)}, u32[]{:S(2)}) copy-start(s32[3]{0:T(128)} %param.9) | copy-start | bytes 40
  308.8 19.7 %all-to-all-start.2 = ((bf16[64,1,10,256]{3,2,1,0:T(8,128)(2,1)}), bf16[64,1,10,256]{3,2,1,0:T(8,128)(2,1)S(1)}, u32[]{:S(2)}, u32[]{:S(2)}) async-start(bf16[64,1,10,256]{3,2,1,0:T(8,128)(2,1)} %reshape.196), calls=%async_computation.2 | async-start | bytes 1048576 | tf_op jit(solution)/shard_map/all_to_all | solution.py:73
Sparse Core Ops, SparseCore 0:
  11.5 115.4 all-gather.7
  128.8 116.4 all-gather.3
  248.8 149.2 all-gather.5
where the time goes:
time: 443 us; the launch traced here: 442 us
  waiting for transfers between devices  330 us (74%)
  local copies, waits for them, and re-layouts  33.7 us (8%)
  starting transfers between devices  31.5 us (7%)
  matrix products  30.5 us (7%)
  between operations  13.9 us (3%)
    all_gather x1, waiting for transfers between devices, body(): gathered = lax.all_gather(tokens, 'fsdp', axis=1, tiled=True)  107 us
    all_gather x1, waiting for transfers between devices, body(): acc_strided = add_rows(lax.all_gather(w_strided, 'seq', axis=0, tiled=True))  101 us
    all_gather x1, waiting for transfers between devices, body(): acc_local = add_rows(lax.all_gather(w_local, 'seq', axis=0, tiled=True))  68.7 us
    all_to_all x1, waiting for transfers between devices, body(): lax.all_to_all(packed, 'seq', split_axis=1, concat_axis=0, tiled=True)  37.1 us
    dot_general x2, matrix products, add_rows(): jnp.dot(gathered, piece.reshape(rows, -1), preferred_element_type=jnp.flo...  22.4 us
    all_to_all x1, starting transfers between devices, body(): lax.all_to_all(marks, 'seq', split_axis=1, concat_axis=0, tiled=True)  15.6 us
    all_gather x1, local copies, waits for them, and re-layouts, body(): acc_local = add_rows(lax.all_gather(w_local, 'seq', axis=0, tiled=True))  15 us
    all_to_all x1, waiting for transfers between devices, body(): lax.all_to_all(result, 'seq', split_axis=0, concat_axis=1, tiled=True)  14.2 us
  transfers between devices with their start and end apart: 6, of which 5 were waited for; matrix products, arithmetic and copies ran while one was open for 7% of the time, Pallas kernels for 0%

commit v1 on v0

--- a/solution.py
+++ b/solution.py
@@ -44,7 +44,11 @@
         return jnp.dot(gathered, piece.reshape(rows, -1), preferred_element_type=jnp.float32)
 
     acc_local = add_rows(lax.all_gather(w_local, "seq", axis=0, tiled=True))
-    acc_strided = add_rows(lax.all_gather(w_strided, "seq", axis=0, tiled=True))
+    acc_strided = add_rows(
+        jnp.concatenate(
+            lax.all_to_all(jnp.stack([w_strided] * lax.axis_size("seq")), "seq", 0, 0), axis=0
+        )
+    )
     packed = acc_strided.astype(jnp.bfloat16).reshape(1, peers, per_peer, 3 * strided_cols)
     marks = valid.astype(jnp.bfloat16).reshape(1, peers, per_peer)
     strided_packed = lax.all_to_all(packed, "seq", split_axis=1, concat_axis=0, tiled=True)

time: 443 us -> 505 us (1.14)
  starting transfers between devices: 31.5 us -> 64.8 us
  local copies, waits for them, and re-layouts: 33.7 us -> 48 us
  waiting for transfers between devices: 330 us -> 344 us
    all_to_all x0 -> x1, waiting for transfers between devices: none -> 221 us  [body(): lax.all_to_all(jnp.stack([w_strided] * lax.axis_size('seq')), 'seq', 0, 0)]
    all_gather x1, waiting for transfers between devices: 107 us -> 0.01 us  [body(): gathered = lax.all_gather(tokens, 'fsdp', axis=1, tiled=True)]
    all_gather x1 -> x0, waiting for transfers between devices: 101 us -> none  [body(): acc_strided = add_rows(lax.all_gather(w_strided, 'seq', axis=0, tiled=True))]
    all_to_all x1, starting transfers between devices: 11.4 us -> 39.1 us  [body(): lax.all_to_all(packed, 'seq', split_axis=1, concat_axis=0, tiled=True)]
    all_to_all x1, waiting for transfers between devices: 14.2 us -> 34.8 us  [body(): lax.all_to_all(result, 'seq', split_axis=0, concat_axis=1, tiled=True)]
    all_to_all x0 -> x1, starting transfers between devices: none -> 15.9 us  [body(): lax.all_to_all(jnp.stack([w_strided] * lax.axis_size('seq')), 'seq', 0, 0)]
    all_to_all x1, starting transfers between devices: 15.6 us -> 4.17 us  [body(): lax.all_to_all(marks, 'seq', split_axis=1, concat_axis=0, tiled=True)]
    all_to_all x0 -> x1, local copies, waits for them, and re-layouts: none -> 11.3 us  [body(): lax.all_to_all(jnp.stack([w_strided] * lax.axis_size('seq')), 'seq', 0, 0)]
  transfers between devices with their start and end apart: 6 -> 6, of which waited for: 5 -> 4; matrix products, arithmetic and copies ran while one was open for 7% -> 9% of each run, Pallas kernels for 0% -> 0%
where the time goes in v1:
time: 505 us; the launch traced here: 503 us
  waiting for transfers between devices  344 us (68%)
  starting transfers between devices  64.8 us (13%)
  local copies, waits for them, and re-layouts  48 us (10%)
  matrix products  30.5 us (6%)
  between operations  14.2 us (3%)
    all_to_all x1, waiting for transfers between devices, body(): lax.all_to_all(jnp.stack([w_strided] * lax.axis_size('seq')), 'seq', 0, 0)  221 us
    all_gather x1, waiting for transfers between devices, body(): acc_local = add_rows(lax.all_gather(w_local, 'seq', axis=0, tiled=True))  59 us
    all_to_all x1, starting transfers between devices, body(): lax.all_to_all(packed, 'seq', split_axis=1, concat_axis=0, tiled=True)  39.1 us
    all_to_all x1, waiting for transfers between devices, body(): lax.all_to_all(result, 'seq', split_axis=0, concat_axis=1, tiled=True)  34.8 us
    all_to_all x1, waiting for transfers between devices, body(): lax.all_to_all(packed, 'seq', split_axis=1, concat_axis=0, tiled=True)  27.6 us
    dot_general x2, matrix products, add_rows(): jnp.dot(gathered, piece.reshape(rows, -1), preferred_element_type=jnp.flo...  22.4 us
    all_to_all x1, starting transfers between devices, body(): lax.all_to_all(jnp.stack([w_strided] * lax.axis_size('seq')), 'seq', 0, 0)  15.9 us
    all_gather x1, local copies, waits for them, and re-layouts, body(): acc_local = add_rows(lax.all_gather(w_local, 'seq', axis=0, tiled=True))  15 us
  transfers between devices with their start and end apart: 6, of which 4 were waited for; matrix products, arithmetic and copies ran while one was open for 9% of the time, Pallas kernels for 0%

profile of v1, /device:TPU:1, one launch (start us, length us, event | category | flops | bytes accessed | tf_op | source)
XLA Modules:
  0.0 502.7 jit_solution(10350871059762677763)
XLA Ops:
  7.9 0.7 all-gather.5.cloned.1.call-update
  8.6 4.6 stack.2
  13.2 15.9 %all-to-all-start = ((bf16[64,80,3,256]{3,1,2,0:T(8,128)(2,1)}), bf16[64,80,3,256]{3,1,2,0:T(8,128)(2,1)}, u32[]{:S(2)}, u32[]{:S(2)}) async-start(bf16[64,80,3,256]{3,1,2,0:T(8,128)(2,1)} %stack.2), calls=%async_computation | async-start | bytes 15728640 | tf_op jit(solution)/shard_map/all_to_all | solution.py:49
  29.2 0.8 reshape.193
  30.0 221.1 %all-to-all-done = bf16[64,80,3,256]{3,1,2,0:T(8,128)(2,1)} async-done(((bf16[64,80,3,256]{3,1,2,0:T(8,128)(2,1)}), bf16[64,80,3,256]{3,1,2,0:T(8,128)(2,1)}, u32[]{:S(2)}, u32[]{:S(2)}) %all-to-all-start) | async-done | bytes 7864352 | tf_op jit(solution)/shard_map/all_to_all | solution.py:49
  251.0 4.2 all-to-all-start.2
  255.2 11.3 %copy.52 = bf16[64,80,3,256]{3,2,1,0:T(4,128)(2,1)} copy(bf16[64,80,3,256]{3,1,2,0:T(8,128)(2,1)} %all-to-all-done) | data formatting | bytes 15728640 | tf_op jit(solution)/shard_map/all_to_all | solution.py:49
  266.5 9.4 %copy.77 = bf16[640,8,3,256]{3,1,2,0:T(8,128)(2,1)} copy(bf16[640,8,3,256]{3,2,1,0:T(4,128)(2,1)} %bitcast.61) | data formatting | bytes 15728640
  275.9 9.6 %convolution_convert_fusion.1 = bf16[640,768]{1,0:T(8,128)(2,1)S(1)} fusion(bf16[640,5120]{1,0:T(8,128)(2,1)} %all-gather.3.cloned.1.call-done, bf16[5120,768]{1,0:T(8,128)(2,1)} %bitcast.63), kind=kOutput, calls=%fused_computation.17 | convolution fusion | flops 5033656320 | bytes 15400960 | tf_op jit(solution)/shard_map/dot_general | solution.py:44
  285.6 1.4 reshape.187
  287.0 39.1 %all-to-all-start.1 = ((bf16[1,64,10,768]{3,2,0,1:T(8,128)(2,1)}), bf16[1,64,10,768]{3,2,0,1:T(8,128)(2,1)S(1)}, u32[]{:S(2)}, u32[]{:S(2)}) async-start(bf16[1,64,10,768]{3,2,0,1:T(8,128)(2,1)} %bitcast.7), calls=%async_computation.1 | async-start | bytes 3145728 | tf_op jit(solution)/shard_map/all_to_all | solution.py:54
  326.5 27.6 %all-to-all-done.1 = bf16[1,64,10,768]{3,2,0,1:T(8,128)(2,1)S(1)} async-done(((bf16[1,64,10,768]{3,2,0,1:T(8,128)(2,1)}), bf16[1,64,10,768]{3,2,0,1:T(8,128)(2,1)S(1)}, u32[]{:S(2)}, u32[]{:S(2)}) %all-to-all-start.1) | async-done | bytes 983072 | tf_op jit(solution)/shard_map/all_to_all | solution.py:54
  356.5 1.0 reshape.194
  357.5 5.5 %all-to-all-start.3 = ((bf16[64,1,10,256]{3,2,1,0:T(8,128)(2,1)}), bf16[64,1,10,256]{3,2,1,0:T(8,128)(2,1)S(1)}, u32[]{:S(2)}, u32[]{:S(2)}) async-start(bf16[64,1,10,256]{3,2,1,0:T(8,128)(2,1)} %reshape.194), calls=%async_computation.3 | async-start | bytes 1048576 | tf_op jit(solution)/shard_map/all_to_all | solution.py:77
  363.2 0.9 fusion.10
  364.1 34.8 %all-to-all-done.3 = bf16[64,1,10,256]{3,2,1,0:T(8,128)(2,1)S(1)} async-done(((bf16[64,1,10,256]{3,2,1,0:T(8,128)(2,1)}), bf16[64,1,10,256]{3,2,1,0:T(8,128)(2,1)S(1)}, u32[]{:S(2)}, u32[]{:S(2)}) %all-to-all-start.3) | async-done | bytes 327712 | tf_op jit(solution)/shard_map/all_to_all | solution.py:77
  398.9 0.8 reshape.191
  399.7 59.0 %all-gather.5.cloned.1.call-done = bf16[5120,3,384]{2,0,1:T(8,128)(2,1)} async-done(((bf16[80,3,384]{2,0,1:T(8,128)(2,1)}), bf16[5120,3,384]{2,0,1:T(8,128)(2,1)}) %all-gather.5.cloned.1.call-update) | async-done | bytes 11796496 | tf_op jit(solution)/shard_map/all_gather | solution.py:46
  458.7 15.0 %copy.47 = bf16[5120,3,384]{0,2,1:T(8,128)(2,1)} copy(bf16[5120,3,384]{2,0,1:T(8,128)(2,1)} %all-gather.5.cloned.1.call-done) | data formatting | bytes 23592960 | tf_op jit(solution)/shard_map/all_gather | solution.py:46
  473.7 12.7 %convolution_convert_fusion = bf16[640,1152]{1,0:T(8,128)(2,1)S(1)} fusion(bf16[640,5120]{1,0:T(8,128)(2,1)} %all-gather.3.cloned.1.call-done, bf16[5120,1152]{0,1:T(8,128)(2,1)} %bitcast.62), kind=kOutput, calls=%fused_computation.5 | convolution fusion | flops 7550484480 | bytes 19824640 | tf_op jit(solution)/shard_map/dot_general | solution.py:44
  486.5 0.9 copy.48
  487.4 3.5 fusion.31
  490.9 4.0 fusion.12
  494.9 1.0 copy.63
  (24 shorter events, 3.7 us)
Async XLA Ops:
  7.2 268.8 %all-gather.3.cloned.1.call-start = ((), (), s32[]{:S(2)}) async-start(), calls=%async_computation.4 | async-start | bytes 8192000 | tf_op jit(solution)/shard_map/all_gather | solution.py:34
  7.9 450.8 %all-gather.5.cloned.1.call-start = ((), (), s32[]{:S(2)}) async-start(), calls=%async_computation.5 | async-start | bytes 11980800 | tf_op jit(solution)/shard_map/all_gather | solution.py:46
  13.2 15.9 %copy-start = (s32[1,640]{1,0:T(1,128)S(1)}, s32[1,640]{1,0:T(1,128)}, u32[]{:S(2)}) copy-start(s32[1,640]{1,0:T(1,128)} %param.8) | copy-start | bytes 7684
  13.2 237.8 %all-to-all-start = ((bf16[64,80,3,256]{3,1,2,0:T(8,128)(2,1)}), bf16[64,80,3,256]{3,1,2,0:T(8,128)(2,1)}, u32[]{:S(2)}, u32[]{:S(2)}) async-start(bf16[64,80,3,256]{3,1,2,0:T(8,128)(2,1)} %stack.2), calls=%async_computation | async-start | bytes 15728640 | tf_op jit(solution)/shard_map/all_to_all | solution.py:49
  251.0 36.0 %all-to-all-start.2 = ((bf16[1,64,10]{2,0,1:T(2,128)(2,1)}), bf16[1,64,10]{2,0,1:T(2,128)(2,1)S(1)}, u32[]{:S(2)}, u32[]{:S(2)}) async-start(bf16[1,64,10]{2,0,1:T(2,128)(2,1)} %reshape.193), calls=%async_computation.2 | async-start | bytes 65536 | tf_op jit(solution)/shard_map/all_to_all | solution.py:55
  287.0 67.0 %all-to-all-start.1 = ((bf16[1,64,10,768]{3,2,0,1:T(8,128)(2,1)}), bf16[1,64,10,768]{3,2,0,1:T(8,128)(2,1)S(1)}, u32[]{:S(2)}, u32[]{:S(2)}) async-start(bf16[1,64,10,768]{3,2,0,1:T(8,128)(2,1)} %bitcast.7), calls=%async_computation.1 | async-start | bytes 3145728 | tf_op jit(solution)/shard_map/all_to_all | solution.py:54
  354.6 8.5 %copy-start.1 = (s32[3]{0:T(128)S(1)}, s32[3]{0:T(128)}, u32[]{:S(2)}) copy-start(s32[3]{0:T(128)} %param.9) | copy-start | bytes 40
  357.5 41.4 %all-to-all-start.3 = ((bf16[64,1,10,256]{3,2,1,0:T(8,128)(2,1)}), bf16[64,1,10,256]{3,2,1,0:T(8,128)(2,1)S(1)}, u32[]{:S(2)}, u32[]{:S(2)}) async-start(bf16[64,1,10,256]{3,2,1,0:T(8,128)(2,1)} %reshape.194), calls=%async_computation.3 | async-start | bytes 1048576 | tf_op jit(solution)/shard_map/all_to_all | solution.py:77
Sparse Core Ops, SparseCore 0:
  9.8 264.1 all-gather.2
  277.5 181.2 all-gather.4
